TPU v7x, 512 devices: a whole 4x4x16 slice. The times are simulated.
512 devices in a mesh: tm: 8 (over y, core), freq: 16 (over z), dish: 4 (over x).
Axes of the slice: x: 4, y: 4, z: 16, core: 2. Of those that a mesh axis runs over, the one named last changes fastest.
Arguments:
- time_data: bfloat16 [64, 512, 4096], P('dish', 'freq', 'tm'), may hold values from -24 to 24
- pointing: bfloat16 [32, 128, 128], P('tm'), may hold values from -0.5 to 0.5
- coverage: int32 [32], P('tm'), may hold values from 0 to 15
- noise_inv: bfloat16 [64, 128, 128], P('dish'), as said below
- gains: float32 [64, 512, 32], P('dish', 'freq', 'tm'), may hold values from 0.1 to 1.9
- prior_inv: float32 [512, 512], replicated, as said below
- precond: float32 [512, 8192], P('freq', ('tm', 'dish')), may hold values from 0.5 to 200
Outputs:
- map_estimate: float32 [512, 8192], P('freq', ('tm', 'dish'))
- residual: float32 [512, 8192], P('freq', ('tm', 'dish'))
Inputs may be any that keep to these rules, and one draw needn't show every extreme that they name: `noise_inv`: each matrix is symmetric with a positive diagonal that dominates its row, and zero where two samples lie more than 16 apart. `prior_inv`: symmetric with a positive diagonal that dominates its row.
All inputs are finite; a program needn't handle non-finite values.
Results may differ from a plain program's by a relative error of at most 0.0045.
Values may be sent and summed in bfloat16 or wider, within the bound.
No kernel may reach another device: no remote copies, remote signals or barrier semaphores. Data moves between devices by JAX's collectives and lax.ppermute only.
A program may use at most 64 MiB of HBM per device.

v0:
```python
import jax
import jax.numpy as jnp
from jax import lax
from jax.sharding import PartitionSpec as P

ITERS = 4


def shifted(block, axis, distance):
    devices = range(lax.axis_size(axis))
    route = [((i - distance) % len(devices), i) for i in devices]
    return lax.ppermute(block, axis, route)


def body(time_data, pointing, coverage, noise_inv, gains, prior_inv, precond):
    highest = lax.Precision.HIGHEST
    channels_dev = precond.shape[0]
    owned_pixels = precond.shape[1]
    blocks_dev = pointing.shape[0]
    dish_count = lax.axis_size("dish")
    owned_tiles = owned_pixels // 128
    region_tiles = owned_tiles * dish_count
    window_tiles = 2 * region_tiles
    tile_count = jnp.arange(owned_tiles, dtype=jnp.int32)
    first_owned = lax.axis_index("dish") * owned_tiles + tile_count
    wanted = jnp.concatenate([first_owned, first_owned + region_tiles])
    own_hot = (coverage[:, None] == wanted[None, :]).astype(jnp.float32)

    def collect(partial_tod):
        summed = lax.psum(partial_tod, "dish")
        tile_part = jnp.einsum(
            "cbt,bti->cbi",
            summed.astype(jnp.bfloat16),
            pointing,
            preferred_element_type=jnp.float32,
        )
        window = jnp.einsum("cbi,bw->cwi", tile_part, own_hot, precision=highest)
        own_part = window[:, :owned_tiles, :].reshape(channels_dev, owned_pixels)
        ahead_part = window[:, owned_tiles:, :].reshape(channels_dev, owned_pixels)
        arrived = shifted(ahead_part, "tm", 1)
        return own_part + arrived

    def energy_of(residual, scaled):
        return lax.psum(jnp.sum(residual * scaled), ("tm", "freq", "dish"))

    series = time_data.reshape(time_data.shape[0], channels_dev, blocks_dev, 128)
    rhs_weighted = jnp.einsum(
        "dcbs,dst->dcbt", series, noise_inv, preferred_element_type=jnp.float32
    )
    right_side = collect(jnp.sum(gains[:, :, :, None] * rhs_weighted, axis=0))
    estimate = jnp.zeros_like(right_side)
    residual = right_side
    scaled = precond * residual
    direction = scaled
    energy_now = energy_of(residual, scaled)
    for iteration in range(ITERS):
        swapped = lax.all_to_all(direction, "freq", split_axis=1, concat_axis=0, tiled=True)
        applied = jnp.dot(prior_inv, swapped, precision=highest, preferred_element_type=jnp.float32)
        region_map = lax.all_gather(direction.astype(jnp.bfloat16), "dish", axis=1, tiled=True)
        following = shifted(region_map, "tm", -1)
        data_window = jnp.concatenate([region_map, following], axis=1)
        tile_maps = data_window.reshape(channels_dev, window_tiles, 128)[:, coverage, :]
        model_tod = jnp.einsum(
            "cbp,bsp->cbs", tile_maps, pointing, preferred_element_type=jnp.float32
        ).astype(jnp.bfloat16)
        weighted = jnp.einsum(
            "cbs,dst->dcbt", model_tod, noise_inv, preferred_element_type=jnp.float32
        )
        mixed_part = jnp.sum((gains * gains)[:, :, :, None] * weighted, axis=0)
        operated = collect(mixed_part) + lax.all_to_all(
            applied, "freq", split_axis=0, concat_axis=1, tiled=True
        )
        curve_sum = lax.psum(jnp.sum(direction * operated), ("tm", "freq", "dish"))
        step_size = energy_now / curve_sum
        estimate = estimate + step_size * direction
        residual = residual - step_size * operated
        if iteration + 1 < ITERS:
            scaled = precond * residual
            energy_next = energy_of(residual, scaled)
            direction = scaled + energy_next / energy_now * direction
            energy_now = energy_next
    return (estimate, residual)


def solution(mesh):
    return jax.shard_map(
        body,
        mesh=mesh,
        in_specs=(
            P("dish", "freq", "tm"),
            P("tm", None, None),
            P("tm"),
            P("dish", None, None),
            P("dish", "freq", "tm"),
            P(),
            P("freq", ("tm", "dish")),
        ),
        out_specs=(P("freq", ("tm", "dish")), P("freq", ("tm", "dish"))),
        check_vma=False,
    )
```

profile of v0, /device:TPU:7, one launch (start us, length us, event | category | flops | bytes accessed | tf_op | source)
XLA Modules:
  0.0 1004.5 jit_solution(7558027323215178378)
XLA Ops:
  0.7 1.7 fusion.8
  2.4 11.0 %psum.91 = bf16[32,4,128]{2,0,1:T(8,128)(2,1)S(1)} all-reduce(f32[32,4,128]{2,0,1:T(8,128)S(1)} %fusion.8), channel_id=1, replica_groups=mesh['tm'=8,'freq'=16,'dish'=4] {'dish'}, use_global_device_ids=true, to_apply=%region_1.0 | all-reduce | flops 16384 | bytes 98304 | tf_op jit(solution)/shard_map/psum | solution.py:30
  14.6 5.3 collective-permute-start
  20.8 3.7 collective-permute-done
  24.5 9.4 all_gather.12
  33.8 7.6 collective-permute-start.1
  41.6 0.7 reshape.134
  42.4 10.5 %all-to-all-start = ((f32[16,1,512]{2,1,0:T(1,128)}), f32[16,1,512]{2,1,0:T(1,128)S(1)}, u32[]{:S(2)}, u32[]{:S(2)}) async-start(f32[16,1,512]{2,1,0:T(1,128)} %reshape.134), calls=%async_computation | async-start | bytes 65536 | tf_op jit(solution)/shard_map/all_to_all | solution.py:57
  54.0 13.7 %psum.93 = bf16[32,4,128]{2,0,1:T(8,128)(2,1)S(1)} all-reduce(f32[32,4,128]{2,0,1:T(8,128)S(1)} %fusion.7), channel_id=1, replica_groups=mesh['tm'=8,'freq'=16,'dish'=4] {'dish'}, use_global_device_ids=true, to_apply=%region_5.0 | all-reduce | flops 16384 | bytes 98304 | tf_op jit(solution)/shard_map/psum | solution.py:30
  68.7 0.7 reduce
  69.7 1.0 convolution_bitcast_fusion.17
  70.8 0.7 reshape.136
  71.6 10.9 %all-to-all-start.1 = ((f32[16,1,512]{2,1,0:T(1,128)}), f32[16,1,512]{2,1,0:T(1,128)S(1)}, u32[]{:S(2)}, u32[]{:S(2)}) async-start(f32[16,1,512]{2,1,0:T(1,128)} %reshape.136), calls=%async_computation.1 | async-start | bytes 65536 | tf_op jit(solution)/shard_map/all_to_all | solution.py:70
  82.6 4.3 collective-permute-start.2
  87.0 6.9 all-to-all-done.1
  93.9 0.7 reduce.1
  94.8 0.6 multiply_reduce_fusion.6
  95.4 103.3 %all-reduce = (f32[]{:T(128)}, f32[]{:T(128)}) all-reduce(f32[]{:T(128)} %get-tuple-element.9, f32[]{:T(128)} %get-tuple-element.8), channel_id=1, replica_groups=mesh['tm'=8,'freq'=16,'dish'=4] {'tm','freq','dish'}, use_global_device_ids=true, to_apply=%region_3.0 | all-reduce | flops 2 | bytes 16 | tf_op jit(solution)/shard_map/psum | solution.py:44
  200.1 0.7 multiply_reduce_fusion.5
  200.7 100.2 %psum.95 = f32[]{:T(128)} all-reduce(f32[]{:T(128)} %get-tuple-element.24), channel_id=1, replica_groups=mesh['tm'=8,'freq'=16,'dish'=4] {'tm','freq','dish'}, use_global_device_ids=true, to_apply=%region_9.0 | all-reduce | flops 1 | bytes 8 | tf_op jit(solution)/shard_map/psum | solution.py:44
  302.3 9.4 all_gather.13
  311.7 3.6 collective-permute-start.3
  315.4 0.7 reshape.138
  316.1 5.4 all-to-all-start.2
  322.7 12.2 %psum.96 = bf16[32,4,128]{2,0,1:T(8,128)(2,1)S(1)} all-reduce(f32[32,4,128]{2,0,1:T(8,128)S(1)} %fusion.6), channel_id=1, replica_groups=mesh['tm'=8,'freq'=16,'dish'=4] {'dish'}, use_global_device_ids=true, to_apply=%region_11.0 | all-reduce | flops 16384 | bytes 98304 | tf_op jit(solution)/shard_map/psum | solution.py:30
  335.3 0.7 reduce.2
  336.3 1.0 convolution_bitcast_fusion.16
  337.4 0.7 reshape.140
  338.1 10.7 %all-to-all-start.3 = ((f32[16,1,512]{2,1,0:T(1,128)}), f32[16,1,512]{2,1,0:T(1,128)S(1)}, u32[]{:S(2)}, u32[]{:S(2)}) async-start(f32[16,1,512]{2,1,0:T(1,128)} %reshape.140), calls=%async_computation.3 | async-start | bytes 65536 | tf_op jit(solution)/shard_map/all_to_all | solution.py:70
  349.0 4.6 collective-permute-start.4
  353.7 6.7 all-to-all-done.3
  360.4 0.7 reduce.3
  361.9 104.5 %psum.97 = f32[]{:T(128)} all-reduce(f32[]{:T(128)} %multiply_reduce_fusion.4), channel_id=1, replica_groups=mesh['tm'=8,'freq'=16,'dish'=4] {'tm','freq','dish'}, use_global_device_ids=true, to_apply=%region_13.0 | all-reduce | flops 1 | bytes 8 | tf_op jit(solution)/shard_map/psum | solution.py:73
  468.3 100.2 %psum.98 = f32[]{:T(128)} all-reduce(f32[]{:T(128)} %get-tuple-element.19), channel_id=1, replica_groups=mesh['tm'=8,'freq'=16,'dish'=4] {'tm','freq','dish'}, use_global_device_ids=true, to_apply=%region_15.0 | all-reduce | flops 1 | bytes 8 | tf_op jit(solution)/shard_map/psum | solution.py:44
  569.9 9.4 all_gather.14
  579.2 3.7 collective-permute-start.5
  583.1 0.7 reshape.142
  583.8 5.4 all-to-all-start.4
  590.4 11.9 %psum.99 = bf16[32,4,128]{2,0,1:T(8,128)(2,1)S(1)} all-reduce(f32[32,4,128]{2,0,1:T(8,128)S(1)} %fusion.5), channel_id=1, replica_groups=mesh['tm'=8,'freq'=16,'dish'=4] {'dish'}, use_global_device_ids=true, to_apply=%region_17.0 | all-reduce | flops 16384 | bytes 98304 | tf_op jit(solution)/shard_map/psum | solution.py:30
  602.7 0.7 reduce.4
  603.7 1.0 convolution_bitcast_fusion.15
  604.8 0.7 reshape.144
  605.6 10.6 %all-to-all-start.5 = ((f32[16,1,512]{2,1,0:T(1,128)}), f32[16,1,512]{2,1,0:T(1,128)S(1)}, u32[]{:S(2)}, u32[]{:S(2)}) async-start(f32[16,1,512]{2,1,0:T(1,128)} %reshape.144), calls=%async_computation.5 | async-start | bytes 65536 | tf_op jit(solution)/shard_map/all_to_all | solution.py:70
  616.3 4.9 collective-permute-start.6
  621.3 6.3 all-to-all-done.5
  627.6 0.7 reduce.5
  629.1 104.9 %psum.100 = f32[]{:T(128)} all-reduce(f32[]{:T(128)} %multiply_reduce_fusion.2), channel_id=1, replica_groups=mesh['tm'=8,'freq'=16,'dish'=4] {'tm','freq','dish'}, use_global_device_ids=true, to_apply=%region_19.0 | all-reduce | flops 1 | bytes 8 | tf_op jit(solution)/shard_map/psum | solution.py:73
  735.4 0.6 multiply_reduce_fusion.1
  736.1 100.2 %psum.101 = f32[]{:T(128)} all-reduce(f32[]{:T(128)} %get-tuple-element.14), channel_id=1, replica_groups=mesh['tm'=8,'freq'=16,'dish'=4] {'tm','freq','dish'}, use_global_device_ids=true, to_apply=%region_21.0 | all-reduce | flops 1 | bytes 8 | tf_op jit(solution)/shard_map/psum | solution.py:44
  837.6 9.4 all_gather.15
  847.0 3.7 collective-permute-start.7
  850.8 0.7 reshape.146
  851.6 5.4 all-to-all-start.6
  858.1 11.9 %psum.102 = bf16[32,4,128]{2,0,1:T(8,128)(2,1)S(1)} all-reduce(f32[32,4,128]{2,0,1:T(8,128)S(1)} %fusion.4), channel_id=1, replica_groups=mesh['tm'=8,'freq'=16,'dish'=4] {'dish'}, use_global_device_ids=true, to_apply=%region_23.0 | all-reduce | flops 16384 | bytes 98304 | tf_op jit(solution)/shard_map/psum | solution.py:30
  870.5 0.7 reduce.6
  871.5 1.0 convolution_bitcast_fusion.14
  872.6 0.7 reshape.148
  873.3 10.6 %all-to-all-start.7 = ((f32[16,1,512]{2,1,0:T(1,128)}), f32[16,1,512]{2,1,0:T(1,128)S(1)}, u32[]{:S(2)}, u32[]{:S(2)}) async-start(f32[16,1,512]{2,1,0:T(1,128)} %reshape.148), calls=%async_computation.7 | async-start | bytes 65536 | tf_op jit(solution)/shard_map/all_to_all | solution.py:70
  884.1 4.9 collective-permute-start.8
  889.1 6.3 all-to-all-done.7
  895.4 0.7 reduce.7
  896.9 105.0 %psum.103 = f32[]{:T(128)} all-reduce(f32[]{:T(128)} %multiply_reduce_fusion), channel_id=1, replica_groups=mesh['tm'=8,'freq'=16,'dish'=4] {'tm','freq','dish'}, use_global_device_ids=true, to_apply=%region_25.0 | all-reduce | flops 1 | bytes 8 | tf_op jit(solution)/shard_map/psum | solution.py:73
  1003.2 0.7 copy.122
  1003.9 0.7 copy.121
  (115 shorter events, 14.9 us)
Async XLA Ops:
  0.6 69.1 %copy-start = (f32[512,512]{1,0:T(8,128)S(1)}, f32[512,512]{1,0:T(8,128)}, u32[]{:S(2)}) copy-start(f32[512,512]{1,0:T(8,128)} %param.12) | copy-start | bytes 3145732
  0.7 12.8 %copy-start.1 = (bf16[4,128,128]{2,1,0:T(8,128)(2,1)S(1)}, bf16[4,128,128]{2,1,0:T(8,128)(2,1)}, u32[]{:S(2)}) copy-start(bf16[4,128,128]{2,1,0:T(8,128)(2,1)} %param.8) | copy-start | bytes 393220
  13.5 0.7 copy-start.4
  14.4 5.5 copy-start.2
  14.6 9.9 collective-permute-start
  19.9 0.8 copy-start.3
  33.8 19.0 %collective-permute-start.1 = (bf16[32,1024]{0,1:T(8,128)(2,1)S(1)}, bf16[32,1024]{0,1:T(8,128)(2,1)S(1)}, u32[]{:S(2)}, u32[]{:S(2)}) collective-permute-start(bf16[32,1024]{0,1:T(8,128)(2,1)S(1)} %all_gather.12), channel_id=1, source_target_pairs={{64,0},{128,64},{192,128},{256,192},{320,256},{384,320},{448,384},... | collective-permute-start | bytes 196616 | tf_op jit(solution)/shard_map/ppermute | solution.py:12
  41.6 12.0 %copy-start.5 = (bf16[16,128,128]{2,1,0:T(8,128)(2,1)S(1)}, bf16[16,128,128]{2,1,0:T(8,128)(2,1)}, u32[]{:S(2)}) copy-start(bf16[16,128,128]{2,1,0:T(8,128)(2,1)} %param.10) | copy-start | bytes 1572868
  42.4 25.8 %all-to-all-start = ((f32[16,1,512]{2,1,0:T(1,128)}), f32[16,1,512]{2,1,0:T(1,128)S(1)}, u32[]{:S(2)}, u32[]{:S(2)}) async-start(f32[16,1,512]{2,1,0:T(1,128)} %reshape.134), calls=%async_computation | async-start | bytes 65536 | tf_op jit(solution)/shard_map/all_to_all | solution.py:57
  71.6 22.4 %all-to-all-start.1 = ((f32[16,1,512]{2,1,0:T(1,128)}), f32[16,1,512]{2,1,0:T(1,128)S(1)}, u32[]{:S(2)}, u32[]{:S(2)}) async-start(f32[16,1,512]{2,1,0:T(1,128)} %reshape.136), calls=%async_computation.1 | async-start | bytes 65536 | tf_op jit(solution)/shard_map/all_to_all | solution.py:70
  82.6 12.2 %collective-permute-start.2 = (f32[32,256]{0,1:T(8,128)S(1)}, f32[32,256]{0,1:T(8,128)S(1)}, u32[]{:S(2)}, u32[]{:S(2)}) collective-permute-start(f32[32,256]{0,1:T(8,128)S(1)} %bitcast.331), channel_id=1, source_target_pairs={{448,0},{0,64},{64,128},{128,192},{192,256},{256,320},{320,384},{3... | collective-permute-start | bytes 98312 | tf_op jit(solution)/shard_map/ppermute | solution.py:12
  311.7 9.8 collective-permute-start.3
  316.1 19.2 %all-to-all-start.2 = ((f32[16,1,512]{2,1,0:T(1,128)}), f32[16,1,512]{2,1,0:T(1,128)S(1)}, u32[]{:S(2)}, u32[]{:S(2)}) async-start(f32[16,1,512]{2,1,0:T(1,128)} %reshape.138), calls=%async_computation.2 | async-start | bytes 65536 | tf_op jit(solution)/shard_map/all_to_all | solution.py:57
  338.1 22.2 %all-to-all-start.3 = ((f32[16,1,512]{2,1,0:T(1,128)}), f32[16,1,512]{2,1,0:T(1,128)S(1)}, u32[]{:S(2)}, u32[]{:S(2)}) async-start(f32[16,1,512]{2,1,0:T(1,128)} %reshape.140), calls=%async_computation.3 | async-start | bytes 65536 | tf_op jit(solution)/shard_map/all_to_all | solution.py:70
  349.0 12.2 %collective-permute-start.4 = (f32[32,256]{0,1:T(8,128)S(1)}, f32[32,256]{0,1:T(8,128)S(1)}, u32[]{:S(2)}, u32[]{:S(2)}) collective-permute-start(f32[32,256]{0,1:T(8,128)S(1)} %bitcast.332), channel_id=1, source_target_pairs={{448,0},{0,64},{64,128},{128,192},{192,256},{256,320},{320,384},{3... | collective-permute-start | bytes 98312 | tf_op jit(solution)/shard_map/ppermute | solution.py:12
  579.2 9.9 collective-permute-start.5
  583.8 18.9 %all-to-all-start.4 = ((f32[16,1,512]{2,1,0:T(1,128)}), f32[16,1,512]{2,1,0:T(1,128)S(1)}, u32[]{:S(2)}, u32[]{:S(2)}) async-start(f32[16,1,512]{2,1,0:T(1,128)} %reshape.142), calls=%async_computation.4 | async-start | bytes 65536 | tf_op jit(solution)/shard_map/all_to_all | solution.py:57
  605.6 22.0 %all-to-all-start.5 = ((f32[16,1,512]{2,1,0:T(1,128)}), f32[16,1,512]{2,1,0:T(1,128)S(1)}, u32[]{:S(2)}, u32[]{:S(2)}) async-start(f32[16,1,512]{2,1,0:T(1,128)} %reshape.144), calls=%async_computation.5 | async-start | bytes 65536 | tf_op jit(solution)/shard_map/all_to_all | solution.py:70
  616.3 12.2 %collective-permute-start.6 = (f32[32,256]{0,1:T(8,128)S(1)}, f32[32,256]{0,1:T(8,128)S(1)}, u32[]{:S(2)}, u32[]{:S(2)}) collective-permute-start(f32[32,256]{0,1:T(8,128)S(1)} %bitcast.333), channel_id=1, source_target_pairs={{448,0},{0,64},{64,128},{128,192},{192,256},{256,320},{320,384},{3... | collective-permute-start | bytes 98312 | tf_op jit(solution)/shard_map/ppermute | solution.py:12
  847.0 9.9 collective-permute-start.7
  851.6 18.9 %all-to-all-start.6 = ((f32[16,1,512]{2,1,0:T(1,128)}), f32[16,1,512]{2,1,0:T(1,128)S(1)}, u32[]{:S(2)}, u32[]{:S(2)}) async-start(f32[16,1,512]{2,1,0:T(1,128)} %reshape.146), calls=%async_computation.6 | async-start | bytes 65536 | tf_op jit(solution)/shard_map/all_to_all | solution.py:57
  873.3 22.1 %all-to-all-start.7 = ((f32[16,1,512]{2,1,0:T(1,128)}), f32[16,1,512]{2,1,0:T(1,128)S(1)}, u32[]{:S(2)}, u32[]{:S(2)}) async-start(f32[16,1,512]{2,1,0:T(1,128)} %reshape.148), calls=%async_computation.7 | async-start | bytes 65536 | tf_op jit(solution)/shard_map/all_to_all | solution.py:70
  884.1 12.2 %collective-permute-start.8 = (f32[32,256]{0,1:T(8,128)S(1)}, f32[32,256]{0,1:T(8,128)S(1)}, u32[]{:S(2)}, u32[]{:S(2)}) collective-permute-start(f32[32,256]{0,1:T(8,128)S(1)} %bitcast.330), channel_id=1, source_target_pairs={{448,0},{0,64},{64,128},{128,192},{192,256},{256,320},{320,384},{3... | collective-permute-start | bytes 98312 | tf_op jit(solution)/shard_map/ppermute | solution.py:12
where the time goes:
time: 1010 us; the launch traced here: 1000 us
  blocking collectives  817 us (81%)
  starting transfers between devices  112 us (11%)
  waiting for transfers between devices  30 us (3%)
  local copies, waits for them, and re-layouts  15.4 us (2%)
  other arithmetic  10.7 us (1%)
  between operations  10.5 us (1%)
    psum x4, blocking collectives, energy_of(): return lax.psum(jnp.sum(residual * scaled), ('tm', 'freq', 'dish'))  404 us
    psum x3, blocking collectives, body(): curve_sum = lax.psum(jnp.sum(direction * operated), ('tm', 'freq', 'dish'))  314 us
    psum x5, blocking collectives, collect(): summed = lax.psum(partial_tod, 'dish')  60.8 us
    all_to_all x4, starting transfers between devices, body(): lax.all_to_all(applied, 'freq', split_axis=0, concat_axis=1, tiled=True)  42.7 us
    ppermute x9, starting transfers between devices, shifted(): return lax.ppermute(block, axis, route)  42.7 us
    all_gather x4, blocking collectives, body(): lax.all_gather(direction.astype(jnp.bfloat16), 'dish', axis=1, tiled=True)  37.5 us
    all_to_all x4, starting transfers between devices, body(): lax.all_to_all(direction, 'freq', split_axis=1, concat_axis=0, tiled=True)  26.6 us
    all_to_all x4, waiting for transfers between devices, body(): lax.all_to_all(applied, 'freq', split_axis=0, concat_axis=1, tiled=True)  26.3 us
  transfers between devices with their start and end apart: 17, of which 5 were waited for; matrix products, arithmetic and copies ran while one was open for 1% of the time, Pallas kernels for 0%

commit v1 on v0

v1 whole, which is shorter than its diff:
```python
import jax
import jax.numpy as jnp
from jax import lax
from jax.experimental import pallas as pl
from jax.experimental.pallas import tpu as pltpu
from jax.sharding import PartitionSpec as P

ITERS = 4
SENT = 254
CODES = 16383.0 / 0.9
DIAGS = 17
F32 = jnp.float32
BF16 = jnp.bfloat16
VMEM = pl.BlockSpec(memory_space=pltpu.VMEM)
SMEM = pl.BlockSpec(memory_space=pltpu.SMEM)


def split(x):
    high = x.astype(BF16)
    return high, (x - high.astype(F32)).astype(BF16)


def encode(gain):
    level = (gain - 1.0) * CODES
    count = jnp.floor(jnp.abs(level) + 0.5)
    place = jnp.floor(count * (1.0 / 128.0))
    value = 1.0 + (count - place * 128.0) * (1.0 / 128.0)
    value = value * 2.0 ** -63
    for step in (64, 32, 16, 8, 4, 2, 1):
        take = place >= step
        value = jnp.where(take, value * 2.0 ** step, value)
        place = jnp.where(take, place - step, place)
    return jnp.where(level < 0.0, -value, value)


def decode(code):
    value = jnp.abs(code)
    count = jnp.zeros_like(code)
    for step in (64, 32, 16, 8, 4, 2, 1):
        take = value >= 2.0 ** (step - 63)
        value = jnp.where(take, value * 2.0 ** -step, value)
        count = jnp.where(take, count + 128.0 * step, count)
    count = (count + (value * 2.0 ** 63 - 1.0) * 128.0) * (1.0 / CODES)
    return jnp.where(code < 0.0, 1.0 - count, 1.0 + count)


def dot_nt(a, b):
    return lax.dot_general(a, b, (((1,), (1,)), ((), ())), preferred_element_type=F32)


def prepare_kernel(data_ref, noise_ref, gain_ref, out_ref, band_ref):
    first_dish = lax.axis_index("dish") * 16
    lane = lax.broadcasted_iota(jnp.int32, (32, 128), 1)
    rows = lax.broadcasted_iota(jnp.int32, (32, 128), 0)
    pick = (lane == 127 - rows).astype(F32).astype(BF16)
    wide = lax.broadcasted_iota(jnp.int32, (128, 128), 1)
    tall = lax.broadcasted_iota(jnp.int32, (128, 128), 0)
    flip = (wide + tall == 127).astype(F32).astype(BF16)
    turned = [jnp.transpose(gain_ref[d]) for d in range(16)]
    rhs = [jnp.zeros((32, 128), F32) for _ in range(4)]
    squares = [jnp.zeros((32, 128), F32) for _ in range(2)]
    for d in range(16):
        noise = noise_ref[d]
        flipped = jnp.dot(noise, flip, preferred_element_type=F32)
        skewed = pltpu.roll(flipped, 0, 1, stride=1, stride_axis=0)
        band_ref[d * 32:(d + 1) * 32, :] = dot_nt(pick, skewed.astype(BF16))
        series = jnp.concatenate([data_ref[d, :, b * 128:(b + 1) * 128] for b in range(4)], axis=0)
        weighted = jnp.dot(series, noise, preferred_element_type=F32)
        for b in range(4):
            gain = jnp.broadcast_to(turned[d][:, b:b + 1], (32, 128))
            rhs[b] = rhs[b] + gain * weighted[b * 32:(b + 1) * 32]
            slot = (b % 2) * 64 + d + first_dish
            squares[b // 2] = jnp.where(lane == slot, gain, squares[b // 2])
    for k in range(DIAGS):
        out_ref[k * 16:(k + 1) * 16, :] = band_ref[pl.ds(k, 16, stride=32), :].astype(BF16)
    for b in range(4):
        high, low = split(rhs[b])
        out_ref[272 + b * 32:304 + b * 32, :] = high
        out_ref[400 + b * 32:432 + b * 32, :] = low
    for h in range(2):
        held = (lane & 63) - first_dish
        held = jnp.logical_and(held >= 0, held < 16)
        out_ref[528 + h * 32:560 + h * 32, :] = jnp.where(held, encode(squares[h]), 0.0).astype(BF16)


def project_kernel(cover_ref, gathered_ref, point_ref, own_ref, square_ref, ahead_ref):
    own = [jnp.zeros((32, 128), F32) for _ in range(2)]
    ahead = [jnp.zeros((32, 128), F32) for _ in range(2)]
    first_tile = lax.axis_index("dish") * 2
    lane = lax.broadcasted_iota(jnp.int32, (16, 128), 1)
    cover_row = jnp.zeros((16, 128), F32)
    for b in range(4):
        total = jnp.zeros((32, 128), F32)
        for j in range(4):
            total = total + gathered_ref[j, 272 + b * 32:304 + b * 32, :].astype(F32)
            total = total + gathered_ref[j, 400 + b * 32:432 + b * 32, :].astype(F32)
        part = jnp.dot(total.astype(BF16), point_ref[b], preferred_element_type=F32)
        tile = cover_ref[b]
        for t in range(2):
            own[t] = own[t] + jnp.where(tile == first_tile + t, part, 0.0)
            ahead[t] = ahead[t] + jnp.where(tile == first_tile + t + 8, part, 0.0)
        cover_row = jnp.where(lane == b, tile.astype(F32), cover_row)
        ahead_ref[192 + b * 128:320 + b * 128, :] = point_ref[b]
    square = jnp.zeros((64, 128), F32)
    for j in range(4):
        square = square + gathered_ref[j, 528:592, :].astype(F32)
    square_ref[...] = square.astype(BF16)
    ahead_ref[128:192, :] = square.astype(BF16)
    for t in range(2):
        own_ref[t * 32:(t + 1) * 32, :] = own[t]
        high, low = split(ahead[t])
        ahead_ref[t * 32:(t + 1) * 32, :] = high
        ahead_ref[64 + t * 32:96 + t * 32, :] = low
    ahead_ref[704:720, :] = cover_row.astype(BF16)


def start_kernel(own_ref, square_ref, arrived_ref, scale_ref, right_ref, out_ref):
    out_ref[64:128, :] = square_ref[...]
    out_ref[128:192, :] = arrived_ref[128:192, :]
    for t in range(2):
        rows = slice(t * 32, (t + 1) * 32)
        cols = slice(t * 128, (t + 1) * 128)
        right = (own_ref[rows, :] + arrived_ref[rows, :].astype(F32)
                 + arrived_ref[64 + t * 32:96 + t * 32, :].astype(F32))
        right_ref[:, cols] = right
        high, low = split(scale_ref[:, cols] * right)
        out_ref[rows, :] = high
        kept = SENT - 192 - t * 32 if t == 1 else 32
        out_ref[192 + t * 32:192 + t * 32 + kept, :] = low[:kept]


def unit(size):
    wide = lax.broadcasted_iota(jnp.int32, (size, size), 1)
    tall = lax.broadcasted_iota(jnp.int32, (size, size), 0)
    return (wide == tall).astype(F32).astype(BF16)


def woven():
    wide = lax.broadcasted_iota(jnp.int32, (128, 128), 1)
    tall = lax.broadcasted_iota(jnp.int32, (128, 128), 0)
    return (wide == (tall & 7) * 16 + (tall >> 3)).astype(F32).astype(BF16)


def weave_point(point, points, points_t, b):
    turn = woven()
    forward = jnp.dot(turn, point, preferred_element_type=F32).astype(BF16)
    flipped = dot_nt(unit(128), forward).astype(BF16)
    for half in range(2):
        points[b, :, half * 128:half * 128 + 128] = forward
        points_t[b, :, half * 128:half * 128 + 128] = flipped


def setup_kernel(noise_ref, prior_ref, point_ref, prior_cat, bands, points, points_t, factor_ref):
    turn = woven()
    prior = prior_ref[...]
    high, low = split(prior)
    prior_cat[0:512, :] = high
    prior_cat[512:1024, :] = low
    prior_cat[1024:1536, :] = high
    for k in range(DIAGS):
        piece = jnp.concatenate([noise_ref[j, k * 16:(k + 1) * 16, :] for j in range(4)] * 2, axis=0)
        bands[k * 128:(k + 1) * 128, :] = dot_nt(turn, piece).astype(BF16)
    for b in range(4):
        weave_point(point_ref[b], points, points_t, b)
    top = jnp.max(jnp.max(jnp.abs(prior), axis=0, keepdims=True), axis=1, keepdims=True)
    diag = jnp.zeros((16, 128), F32)
    for j in range(4):
        diag = diag + noise_ref[j, 0:16, :].astype(F32)
    level = jnp.sum(jnp.sum(diag, axis=0, keepdims=True), axis=1, keepdims=True) * (1.0 / 128.0)
    factor_ref[...] = jnp.broadcast_to(1.0 / (512.0 * (top + level)), (8, 128))


def choose_own():
    lane = lax.broadcasted_iota(jnp.int32, (32, 512), 1)
    line = lax.broadcasted_iota(jnp.int32, (32, 512), 0)
    return (lane == line + lax.axis_index("freq") * 32).astype(F32).astype(BF16)


def build_mixer(covers, bands, squares, mixer):
    first_tile = lax.axis_index("dish") * 2

    @pl.loop(0, 8)
    def _(b):
        cover = covers[b] - first_tile

        @pl.when(jnp.logical_and(cover >= 0, cover < 2))
        def _():
            square = squares[b]
            for k in range(DIAGS):
                mixer[b, k] = jnp.dot(bands[k * 128:(k + 1) * 128, :], square, preferred_element_type=F32)


def apply_mixer(b, mixer, model, mixed):
    @pl.loop(0, 4)
    def _(group):
        cols = pl.ds(pl.multiple_of(group * 128, 128), 128)
        near, sums = {}, {}

        def at(i):
            if i not in near:
                value = model[(i % 16) * 8:(i % 16) * 8 + 8, cols]
                near[i] = pltpu.roll(value, 7, 0) if i >= 16 else value
            return near[i]

        for i in range(16):
            own = at(i)
            weight = mixer[b, 0, i * 8:(i + 1) * 8, cols]
            total = weight * own
            if i in sums:
                total = total + sums[i]
            for k in range(1, DIAGS):
                weight = mixer[b, k, i * 8:(i + 1) * 8, cols]
                total = total + weight * at(i + k)
                spill = weight * own
                sums[i + k] = sums[i + k] + spill if i + k in sums else spill
            mixed[i * 8:(i + 1) * 8, cols] = total
        for i in range(16):
            mixed[i * 8:(i + 1) * 8, cols] += pltpu.roll(sums[16 + i], 1, 0)


def square_form(b, mixer, model):
    def step(group, running):
        cols = pl.ds(pl.multiple_of(group * 128, 128), 128)
        near = {}

        def at(i):
            if i not in near:
                value = model[(i % 16) * 8:(i % 16) * 8 + 8, cols]
                near[i] = pltpu.roll(value, 7, 0) if i >= 16 else value
            return near[i]

        for i in range(16):
            own = at(i)
            value = mixer[b, 1, i * 8:(i + 1) * 8, cols] * at(i + 1)
            for k in range(2, DIAGS):
                value = value + mixer[b, k, i * 8:(i + 1) * 8, cols] * at(i + k)
            value = 2.0 * value + mixer[b, 0, i * 8:(i + 1) * 8, cols] * own
            running = running + value * own
        return running

    return lax.fori_loop(0, 4, step, jnp.zeros((8, 128), F32))


def krylov_kernel(cover_ref, bands, gathered_ref, scales_ref, prior_cat, point_ref, flip_ref, factor_ref, arrived_ref,
                  moment_ref, covers, scale, squares, points, points_t, start_ref,
                  mixer, vector_cat, vector_stack, vector, image, scale_rows,
                  stage, stage_low, model, mixed, mixed_stack, forms):
    first_tile = lax.axis_index("dish") * 2
    eye = unit(128)
    for q in range(4):
        for f in range(16):
            stage[f * 32:(f + 1) * 32, :] = gathered_ref[f, 64 + q * 32:96 + q * 32, :]
        gain = decode(stage[...].astype(F32))
        high, low = split(gain * gain)
        high, low = dot_nt(eye, high).astype(BF16), dot_nt(eye, low).astype(BF16)
        for side in range(2):
            squares[2 * q + side, 0:64, :] = high[side * 64:side * 64 + 64]
            squares[2 * q + side, 64:128, :] = low[side * 64:side * 64 + 64]
    stage_low[...] = jnp.zeros_like(stage_low)
    for t in range(2):
        kept = SENT - 192 - t * 32 if t == 1 else 32
        if t == 1:
            stage_low[...] = jnp.zeros_like(stage_low)
        for f in range(16):
            stage[f * 32:(f + 1) * 32, :] = gathered_ref[f, t * 32:(t + 1) * 32, :]
            stage_low[f * 32:f * 32 + kept, :] = gathered_ref[f, 192 + t * 32:192 + t * 32 + kept, :]
        vector[t * 128:(t + 1) * 128, :] = dot_nt(eye, stage[...]) + dot_nt(eye, stage_low[...])
    start_ref[...] = vector[...]
    for f in range(16):
        scale_rows[f * 32:(f + 1) * 32, :] = scales_ref[f, 0:32, :]
    scale[...] = jnp.transpose(scale_rows[...])
    row = arrived_ref[704:720, :].astype(F32)[0:1, :]
    spot = lax.broadcasted_iota(jnp.int32, (1, 128), 1)
    for b in range(4):
        covers[b] = cover_ref[b]
        covers[4 + b] = jnp.sum(jnp.where(spot == b, row, 0.0)).astype(jnp.int32) - 8
        points[b] = point_ref[b]
        points_t[b] = flip_ref[b]
        weave_point(arrived_ref[192 + b * 128:320 + b * 128, :], points, points_t, 4 + b)
    factor = factor_ref[0:1, 0:1]
    build_mixer(covers, bands, squares, mixer)

    def total(a, b):
        both = a * b
        both = both[:, 0:128] + both[:, 128:256] + (both[:, 256:384] + both[:, 384:512])
        return jnp.sum(both, axis=0, keepdims=True)

    forms[...] = jnp.zeros_like(forms)
    sums = [total(vector[...] * vector[...], 1.0 / scale[...])]
    for iteration in range(ITERS):
        last = iteration + 1 == ITERS
        high, low = split(vector[...])
        vector_cat[:, 0:512] = high
        vector_cat[:, 512:1024] = high
        vector_cat[:, 1024:1536] = low
        for t in range(2):
            vector_stack[t, 0:128, :] = high[t * 128:(t + 1) * 128]
            vector_stack[t, 128:256, :] = low[t * 128:(t + 1) * 128]
        image[...] = jnp.dot(vector_cat[...], prior_cat[...], preferred_element_type=F32)

        @pl.loop(0, 8)
        def _(b):
            cover = covers[b] - first_tile

            @pl.when(jnp.logical_and(cover >= 0, cover < 2))
            def _():
                model[...] = jnp.dot(points[b], vector_stack[cover], preferred_element_type=F32)
                if last:
                    forms[...] += square_form(b, mixer, model)
                else:
                    apply_mixer(b, mixer, model, mixed)
                    high, low = split(mixed[...])
                    mixed_stack[0:128, :] = high
                    mixed_stack[128:256, :] = low
                    rows = pl.ds(pl.multiple_of(cover * 128, 128), 128)
                    image[rows, :] += jnp.dot(points_t[b], mixed_stack[...], preferred_element_type=F32)

        result = image[...]
        found = total(vector[...], result)
        if last:
            found = found + jnp.sum(forms[...], axis=0, keepdims=True)
        sums.append(found)
        if not last:
            following = scale[...] * result * factor
            vector[...] = following
            sums.append(total(following, result))
    sums = jnp.concatenate(sums, axis=0)
    for i in range(32):
        moment_ref[i] = sums


def steps_of(moments_ref, factor):
    sums = moments_ref[0]
    for i in range(1, 32):
        sums = sums + moments_ref[i]
    sums = jnp.broadcast_to(jnp.sum(sums, axis=1, keepdims=True), (8, 128))
    mu = [sums[n:n + 1, :] for n in range(8)]
    one = jnp.ones((1, 128), F32)
    norm = [one / jnp.sqrt(mu[2 * i + 1]) for i in range(4)]
    system = [[mu[i + j + 1] * norm[i] * norm[j] for j in range(4)] for i in range(4)]
    target = [(mu[0] if i == 0 else mu[i] * factor) * norm[i] for i in range(4)]
    lower = [[None] * 4 for _ in range(4)]
    inverse, pivot, forward = [None] * 4, [None] * 4, [None] * 4
    alphas, energies = [], []
    lead, sound = one, one > 0.0
    for i in range(4):
        for j in range(i):
            value = system[i][j]
            for m in range(j):
                value = value - lower[i][m] * lower[j][m] * pivot[m]
            lower[i][j] = value * inverse[j]
        value, aim = system[i][i], target[i]
        for m in range(i):
            value = value - lower[i][m] * lower[i][m] * pivot[m]
            aim = aim - lower[i][m] * forward[m]
        sound = jnp.logical_and(sound, value > 1e-6)
        pivot[i] = value
        inverse[i] = jnp.where(sound, one / value, 0.0)
        forward[i] = aim
        scaled = jnp.where(sound, lead / norm[i], one)
        alpha = aim * inverse[i] / scaled
        alphas.append(alpha)
        energies.append(alpha * scaled * scaled * pivot[i])
        sound = jnp.logical_and(sound, energies[i] > 0.0)
        lead = jnp.where(sound, -lead * alpha / factor, one)
        if i > 0:
            energies[i - 1] = jnp.where(sound, energies[i] / energies[i - 1], 0.0)
    return alphas, energies[:3]


def replay_kernel(covers, moments_ref, factor_ref, bands, squares, points, points_t, prior_cat, start_ref, scale,
                  right_ref, estimate_ref, residual_ref,
                  mixer, vector_cat, vector, carried, image, estimate, removed, model, mixed):
    first_tile = lax.axis_index("dish") * 2
    mine = choose_own()
    alphas, betas = steps_of(moments_ref, factor_ref[0:1, :])
    alphas = [value[0:1, 0:1] for value in alphas]
    betas = [value[0:1, 0:1] for value in betas]
    build_mixer(covers, bands, squares, mixer)
    vector[...] = start_ref[...]
    carried[...] = start_ref[...]
    for iteration in range(ITERS):
        high, low = split(vector[...])
        vector_cat[:, 0:512] = high
        vector_cat[:, 512:1024] = high
        vector_cat[:, 1024:1536] = low
        image[...] = jnp.dot(vector_cat[...], prior_cat[...], preferred_element_type=F32)

        @pl.loop(0, 8)
        def _(b):
            cover = covers[b] - first_tile

            @pl.when(jnp.logical_and(cover >= 0, cover < 2))
            def _():
                rows = pl.ds(pl.multiple_of(cover * 128, 128), 128)
                made = jnp.dot(points[b, :, 0:128], vector_cat[rows, 0:512], preferred_element_type=F32)
                model[...] = made.astype(BF16).astype(F32)
                apply_mixer(b, mixer, model, mixed)
                half = mixed[...].astype(BF16)
                image[rows, :] += jnp.dot(points_t[b, :, 0:128], half, preferred_element_type=F32)

        alpha = alphas[iteration]
        result = alpha * image[...]
        if iteration == 0:
            estimate[...] = alpha * vector[...]
            removed[...] = result
        else:
            estimate[...] = estimate[...] + alpha * vector[...]
            removed[...] = removed[...] + result
        if iteration + 1 < ITERS:
            moved = carried[...] - scale[...] * result
            carried[...] = moved
            vector[...] = moved + betas[iteration] * vector[...]
    high, low = split(estimate[...])
    estimate_ref[...] = dot_nt(mine, high) + dot_nt(mine, low)
    high, low = split(removed[...])
    residual_ref[...] = right_ref[...] - (dot_nt(mine, high) + dot_nt(mine, low))


def shape(dims, kind):
    return jax.ShapeDtypeStruct(dims, kind)


def body(time_data, pointing, coverage, noise_inv, gains, prior_inv, precond):
    spread = lax.all_gather(jnp.concatenate([precond, precond]), "freq", axis=0)
    packed = pl.pallas_call(
        prepare_kernel,
        out_shape=shape((592, 128), BF16),
        in_specs=[VMEM, VMEM, VMEM],
        out_specs=VMEM,
        scratch_shapes=[pltpu.VMEM((512, 128), F32)],
        name="prepare",
    )(time_data, noise_inv, jnp.swapaxes(gains, 1, 2))
    over_dish = lax.all_gather(packed, "dish", axis=0)
    own, square, ahead = pl.pallas_call(
        project_kernel,
        out_shape=(shape((64, 128), F32), shape((64, 128), BF16), shape((720, 128), BF16)),
        in_specs=[SMEM, VMEM, VMEM],
        out_specs=(VMEM, VMEM, VMEM),
        name="project",
    )(coverage, over_dish, pointing)
    count = lax.axis_size("tm")
    arrived = lax.ppermute(ahead, "tm", [(i, (i + 1) % count) for i in range(count)])
    prior_cat, bands, points, points_t, factor = pl.pallas_call(
        setup_kernel,
        out_shape=(shape((1536, 512), BF16), shape((DIAGS * 128, 128), BF16), shape((4, 128, 256), BF16),
                   shape((4, 128, 256), BF16), shape((8, 128), F32)),
        in_specs=[VMEM] * 3,
        out_specs=(VMEM,) * 5,
        cost_estimate=pl.CostEstimate(flops=200_000_000, bytes_accessed=6_000_000, transcendentals=0),
        name="setup",
    )(over_dish, prior_inv, pointing)
    right, packed = pl.pallas_call(
        start_kernel,
        out_shape=(shape((32, 256), F32), shape((SENT, 128), BF16)),
        in_specs=[VMEM] * 4,
        out_specs=(VMEM, VMEM),
        name="start",
    )(own, square, arrived, precond)
    over_freq = lax.all_gather(packed, "freq", axis=0)
    whole = (256, 512)
    moments, covers, scale, squares, points, points_t, first = pl.pallas_call(
        krylov_kernel,
        out_shape=(shape((32, 8, 128), F32), shape((8,), jnp.int32), shape(whole, F32), shape((8, 128, 512), BF16),
                   shape((8, 128, 256), BF16), shape((8, 128, 256), BF16), shape(whole, F32)),
        in_specs=[SMEM] + [VMEM] * 8,
        out_specs=(VMEM, SMEM) + (VMEM,) * 5,
        scratch_shapes=[
            pltpu.VMEM((8, DIAGS, 128, 512), F32),
            pltpu.VMEM((256, 1536), BF16),
            pltpu.VMEM((2, 256, 512), BF16),
            pltpu.VMEM(whole, F32),
            pltpu.VMEM(whole, F32),
            pltpu.VMEM((512, 256), F32),
            pltpu.VMEM((512, 128), BF16),
            pltpu.VMEM((512, 128), BF16),
            pltpu.VMEM((128, 512), F32),
            pltpu.VMEM((128, 512), F32),
            pltpu.VMEM(whole, BF16),
            pltpu.VMEM((8, 128), F32),
        ],
        compiler_params=pltpu.CompilerParams(vmem_limit_bytes=54 * 1024 * 1024),
        name="krylov",
    )(coverage, bands, over_freq, spread, prior_cat, points, points_t, factor, arrived)
    shared = lax.all_to_all(moments, ("tm", "dish"), split_axis=0, concat_axis=0)
    return tuple(pl.pallas_call(
        replay_kernel,
        out_shape=(shape((32, 256), F32), shape((32, 256), F32)),
        in_specs=[SMEM] + [VMEM] * 10,
        out_specs=(VMEM, VMEM),
        scratch_shapes=[
            pltpu.VMEM((8, DIAGS, 128, 512), F32),
            pltpu.VMEM((256, 1536), BF16),
            pltpu.VMEM(whole, F32),
            pltpu.VMEM(whole, F32),
            pltpu.VMEM(whole, F32),
            pltpu.VMEM(whole, F32),
            pltpu.VMEM(whole, F32),
            pltpu.VMEM((128, 512), F32),
            pltpu.VMEM((128, 512), F32),
        ],
        compiler_params=pltpu.CompilerParams(vmem_limit_bytes=54 * 1024 * 1024),
        name="replay",
    )(covers, shared, factor, bands, squares, points, points_t, prior_cat, first, scale, right))


def solution(mesh):
    return jax.shard_map(
        body,
        mesh=mesh,
        in_specs=(
            P("dish", "freq", "tm"),
            P("tm", None, None),
            P("tm"),
            P("dish", None, None),
            P("dish", "freq", "tm"),
            P(),
            P("freq", ("tm", "dish")),
        ),
        out_specs=(P("freq", ("tm", "dish")), P("freq", ("tm", "dish"))),
        check_vma=False,
    )
```

time: 1010 us -> 146 us (0.14)
  blocking collectives: 817 us -> 65.8 us
  starting transfers between devices: 112 us -> 4.21 us
  Pallas kernels: 0 us -> 55.8 us
  waiting for transfers between devices: 30 us -> 3.56 us
  local copies, waits for them, and re-layouts: 15.4 us -> 0.68 us
    psum x12 -> x0, blocking collectives: 779 us -> none  [the longest x4 404 us: energy_of(): return lax.psum(jnp.sum(residual * scaled), ('tm', 'freq', 'dish'))]
    all_to_all x8 -> x0, starting transfers between devices: 69.3 us -> none  [the longest x4 42.7 us: body(): lax.all_to_all(applied, 'freq', split_axis=0, concat_axis=1, tiled=True)]
    pallas_call x0 -> x6, Pallas kernels: none -> 55.8 us  [the longest x1 23.9 us: body(): pl.pallas_call(krylov_kernel, out_shape=(shape((32, 8, 128), F32), shape(...]
    ppermute x9 -> x1, starting transfers between devices: 42.7 us -> 4.17 us  [body(): lax.ppermute(ahead, 'tm', [(i, (i + 1) % count) for i in range(count)])]
    all_to_all x8 -> x0, waiting for transfers between devices: 26.3 us -> none  [the longest x4 26.3 us: body(): lax.all_to_all(applied, 'freq', split_axis=0, concat_axis=1, tiled=True)]
    all_to_all x0 -> x1, blocking collectives: none -> 16.2 us  [body(): lax.all_to_all(moments, ('tm', 'dish'), split_axis=0, concat_axis=0)]
    all_gather x4 -> x2, blocking collectives: 37.5 us -> 49.6 us  [the longest x1 38 us: body(): over_freq = lax.all_gather(packed, 'freq', axis=0)]
  transfers between devices with their start and end apart: 17 -> 2, of which waited for: 5 -> 2; matrix products, arithmetic and copies ran while one was open for 1% -> 0% of each run, Pallas kernels for 0% -> 7%
where the time goes in v1:
time: 146 us
  blocking collectives  65.8 us (45%)
  Pallas kernels  55.8 us (38%)
  between operations  14 us (10%)
  starting transfers between devices  4.21 us (3%)
  waiting for transfers between devices  3.56 us (2%)
  other arithmetic  1.46 us (1%)
    all_gather x1, blocking collectives, body(): over_freq = lax.all_gather(packed, 'freq', axis=0)  38 us
    pallas_call x1, Pallas kernels, body(): pl.pallas_call(krylov_kernel, out_shape=(shape((32, 8, 128), F32), shape(...  23.9 us
    pallas_call x1, Pallas kernels, body(): pl.pallas_call(replay_kernel, out_shape=(shape((32, 256), F32), shape((32...  21.9 us
    all_to_all x1, blocking collectives, body(): lax.all_to_all(moments, ('tm', 'dish'), split_axis=0, concat_axis=0)  16.2 us
    all_gather x1, blocking collectives, body(): over_dish = lax.all_gather(packed, 'dish', axis=0)  11.6 us
    ppermute x1, starting transfers between devices, body(): lax.ppermute(ahead, 'tm', [(i, (i + 1) % count) for i in range(count)])  4.17 us
    pallas_call x1, Pallas kernels, body(): pl.pallas_call(setup_kernel, out_shape=(shape((1536, 512), BF16), shape((...  3.58 us
  transfers between devices with their start and end apart: 2, of which 2 were waited for; matrix products, arithmetic and copies ran while one was open for 0% of the time, Pallas kernels for 7%

profile of v1, /device:TPU:7, one launch (start us, length us, event | category | flops | bytes accessed | tf_op | source)
XLA Modules:
  0.0 145.5 jit_solution(18181219669747632760)
XLA Ops:
  7.2 0.0 all-gather.6.cloned.1.call-start
  7.2 1.5 %pad_maximum_fusion = f32[64,256]{1,0:T(8,128)} fusion(f32[32,256]{1,0:T(8,128)} %scale_ref.1), kind=kLoop, calls=%fused_computation | loop fusion | flops 16384 | bytes 98304 | tf_op jit(solution)/shard_map/concatenate | solution.py:425
  8.7 0.0 all-gather.6.cloned.1.call-update
  8.7 2.9 %prepare.1 = bf16[592,128]{1,0:T(8,128)(2,1)} custom-call(bf16[16,32,512]{2,1,0:T(8,128)(2,1)} %data_ref.1, bf16[16,128,128]{2,1,0:T(8,128)(2,1)} %noise_ref.1, f32[16,4,32]{2,1,0:T(4,128)} %bitcast.8), custom_call_target="tpu_custom_call" | custom-call | tf_op jit(solution)/shard_map/prepare/pallas_call | solution.py:426
  11.6 11.6 %all-gather = bf16[2368,128]{1,0:T(8,128)(2,1)} all-gather(bf16[592,128]{1,0:T(8,128)(2,1)} %prepare.1), channel_id=2, replica_groups=mesh['tm'=8,'freq'=16,'dish'=4] {'dish'}, dimensions={0}, use_global_device_ids=true | all-gather | bytes 757760 | tf_op jit(solution)/shard_map/all_gather | solution.py:434
  23.2 2.0 %project.1 = (f32[64,128]{1,0:T(8,128)}, bf16[64,128]{1,0:T(8,128)(2,1)}, bf16[720,128]{1,0:T(8,128)(2,1)}) custom-call(s32[4]{0:T(128)} %cover_ref.3, bf16[4,592,128]{2,1,0:T(8,128)(2,1)} %bitcast.4, bf16[4,128,128]{2,1,0:T(8,128)(2,1)} %point_ref.3), custom_call_target="tpu_custom_call" | custom-call | tf_op jit(solution)/shard_map/project/pallas_call | solution.py:435
  25.1 4.2 %collective-permute-start = (bf16[720,128]{1,0:T(8,128)(2,1)}, bf16[720,128]{1,0:T(8,128)(2,1)S(1)}, u32[]{:S(2)}, u32[]{:S(2)}) collective-permute-start(bf16[720,128]{1,0:T(8,128)(2,1)} %get-tuple-element.22), channel_id=1, source_target_pairs={{0,64},{64,128},{128,192},{192,256},{256,320},{320,384},{384,448},... | collective-permute-start | bytes 552968 | tf_op jit(solution)/shard_map/ppermute | solution.py:443
  29.3 3.6 %setup.1 = (bf16[1536,512]{1,0:T(8,128)(2,1)}, bf16[2176,128]{1,0:T(8,128)(2,1)}, bf16[4,128,256]{2,1,0:T(8,128)(2,1)}, bf16[4,128,256]{2,1,0:T(8,128)(2,1)}, f32[8,128]{1,0:T(8,128)}) custom-call(bf16[4,592,128]{2,1,0:T(8,128)(2,1)} %bitcast.5, f32[512,512]{1,0:T(8,128)} %prior_ref.1, bf16[4,128,128]{2,1,0:T(8,128)(2,1)} %point_ref.3), custom_call_target="tpu_custom_call" | custom-call | flops 200000000 | bytes 6000000 | tf_op jit(solution)/shard_map/setup/pallas_call | solution.py:444
  32.9 1.1 collective-permute-done.arrived_ref
  34.0 0.0 copy-start
  34.0 0.7 copy-done
  34.7 1.6 %start.1 = (f32[32,256]{1,0:T(8,128)}, bf16[254,128]{1,0:T(8,128)(2,1)}) custom-call(f32[64,128]{1,0:T(8,128)} %get-tuple-element.20.own_ref, bf16[64,128]{1,0:T(8,128)(2,1)} %get-tuple-element.21.square_ref, bf16[720,128]{1,0:T(8,128)(2,1)} %copy-done, f32[32,256]{1,0:T(8,128)} %scale_ref.1), custom_call_target="tpu_custom_call" | custom-call | tf_op jit(solution)/shard_map/start/pallas_call | solution.py:453
  36.3 38.0 %all-gather.3.gathered_ref = bf16[16,254,128]{2,1,0:T(8,128)(2,1)} all-gather(bf16[1,254,128]{2,1,0:T(8,128)(2,1)} %bitcast.7), channel_id=3, replica_groups=mesh['tm'=8,'freq'=16,'dish'=4] {'freq'}, dimensions={0}, use_global_device_ids=true | all-gather | bytes 1105408 | tf_op jit(solution)/shard_map/all_gather | solution.py:460
  74.3 2.4 %all-gather.6.cloned.1.call-done = f32[1024,256]{1,0:T(8,128)} async-done(((f32[64,256]{1,0:T(8,128)}), f32[1024,256]{1,0:T(8,128)}) %all-gather.6.cloned.1.call-update) | async-done | bytes 1048592 | tf_op jit(solution)/shard_map/all_gather | solution.py:425
  76.7 23.9 %krylov.1 = (f32[32,8,128]{2,1,0:T(8,128)}, s32[8]{0:T(128)}, f32[256,512]{1,0:T(8,128)}, bf16[8,128,512]{2,1,0:T(8,128)(2,1)}, bf16[8,128,256]{2,1,0:T(8,128)(2...) custom-call(s32[4]{0:T(128)} %cover_ref.3, bf16[2176,128]{1,0:T(8,128)(2,1)} %get-tuple-element.19.bands, ...), custom_call_target="tpu_custom_call" | custom-call | tf_op jit(solution)/shard_map/krylov/pallas_call | solution.py:462
  100.6 16.2 %all_to_all.5.moments_ref = f32[32,8,128]{2,1,0:T(8,128)} all-to-all(f32[32,8,128]{2,1,0:T(8,128)} %get-tuple-element.29), channel_id=1, replica_groups=mesh['tm'=8,'freq'=16,'dish'=4] {'tm','dish'}, dimensions={0} | all-to-all | bytes 262144 | tf_op jit(solution)/shard_map/all_to_all | solution.py:485
  116.8 21.9 %replay.1 = (f32[32,256]{1,0:T(8,128)}, f32[32,256]{1,0:T(8,128)}) custom-call(s32[8]{0:T(128)} %get-tuple-element.28.covers, f32[32,8,128]{2,1,0:T(8,128)} %all_to_all.5.moments_ref, f32[8,128]{1,0:T(8,128)} %get-tuple-element.27.factor_ref, bf16[2176,128]{1,0:T(8,128)(2,1)} %get-tuple-element.19.bands, bf16[8,128,512]{2,1,0:T(8,128)(2,1)} %get-tuple-element.30.squares, ...), custom_call_target="tpu_custom_call" | custom-call | tf_op jit(solution)/shard_map/replay/pallas_call | solution.py:486
Async XLA Ops:
  7.2 69.6 %all-gather.6.cloned.1.call-start = ((), (), s32[]{:S(2)}) async-start(), calls=%async_computation.1 | async-start | bytes 1114112 | tf_op jit(solution)/shard_map/all_gather | solution.py:425
  25.1 8.9 %collective-permute-start = (bf16[720,128]{1,0:T(8,128)(2,1)}, bf16[720,128]{1,0:T(8,128)(2,1)S(1)}, u32[]{:S(2)}, u32[]{:S(2)}) collective-permute-start(bf16[720,128]{1,0:T(8,128)(2,1)} %get-tuple-element.22), channel_id=1, source_target_pairs={{0,64},{64,128},{128,192},{192,256},{256,320},{320,384},{384,448},... | collective-permute-start | bytes 552968 | tf_op jit(solution)/shard_map/ppermute | solution.py:443
  34.0 0.7 copy-start
Sparse Core Ops, SparseCore 0:
  10.1 66.6 all-gather.5

commit v2 on v1

--- a/solution.py
+++ b/solution.py
@@ -187,7 +187,11 @@
         def _():
             square = squares[b]
             for k in range(DIAGS):
-                mixer[b, k] = jnp.dot(bands[k * 128:(k + 1) * 128, :], square, preferred_element_type=F32)
+                made = jnp.dot(bands[k * 128:(k + 1) * 128, :], square, preferred_element_type=F32)
+                for group in range(4):
+                    for i in range(16):
+                        row = (i * DIAGS + k) * 8
+                        mixer[b, group, row:row + 8, :] = made[i * 8:(i + 1) * 8, group * 128:(group + 1) * 128]
 
 
 def apply_mixer(b, mixer, model, mixed):
@@ -204,12 +208,12 @@
 
         for i in range(16):
             own = at(i)
-            weight = mixer[b, 0, i * 8:(i + 1) * 8, cols]
+            weight = mixer[b, group, i * DIAGS * 8:i * DIAGS * 8 + 8, :]
             total = weight * own
             if i in sums:
                 total = total + sums[i]
             for k in range(1, DIAGS):
-                weight = mixer[b, k, i * 8:(i + 1) * 8, cols]
+                weight = mixer[b, group, (i * DIAGS + k) * 8:(i * DIAGS + k) * 8 + 8, :]
                 total = total + weight * at(i + k)
                 spill = weight * own
                 sums[i + k] = sums[i + k] + spill if i + k in sums else spill
@@ -231,21 +235,18 @@
 
         for i in range(16):
             own = at(i)
-            value = mixer[b, 1, i * 8:(i + 1) * 8, cols] * at(i + 1)
+            value = mixer[b, group, i * DIAGS * 8 + 8:i * DIAGS * 8 + 16, :] * at(i + 1)
             for k in range(2, DIAGS):
-                value = value + mixer[b, k, i * 8:(i + 1) * 8, cols] * at(i + k)
-            value = 2.0 * value + mixer[b, 0, i * 8:(i + 1) * 8, cols] * own
+                value = value + mixer[b, group, (i * DIAGS + k) * 8:(i * DIAGS + k) * 8 + 8, :] * at(i + k)
+            value = 2.0 * value + mixer[b, group, i * DIAGS * 8:i * DIAGS * 8 + 8, :] * own
             running = running + value * own
         return running
 
     return lax.fori_loop(0, 4, step, jnp.zeros((8, 128), F32))
 
 
-def krylov_kernel(cover_ref, bands, gathered_ref, scales_ref, prior_cat, point_ref, flip_ref, factor_ref, arrived_ref,
-                  moment_ref, covers, scale, squares, points, points_t, start_ref,
-                  mixer, vector_cat, vector_stack, vector, image, scale_rows,
-                  stage, stage_low, model, mixed, mixed_stack, forms):
-    first_tile = lax.axis_index("dish") * 2
+def assemble_kernel(cover_ref, gathered_ref, point_ref, flip_ref, arrived_ref,
+                    covers, squares, points, points_t, start_ref, stage, stage_low):
     eye = unit(128)
     for q in range(4):
         for f in range(16):
@@ -256,19 +257,13 @@
         for side in range(2):
             squares[2 * q + side, 0:64, :] = high[side * 64:side * 64 + 64]
             squares[2 * q + side, 64:128, :] = low[side * 64:side * 64 + 64]
-    stage_low[...] = jnp.zeros_like(stage_low)
     for t in range(2):
         kept = SENT - 192 - t * 32 if t == 1 else 32
-        if t == 1:
-            stage_low[...] = jnp.zeros_like(stage_low)
+        stage_low[...] = jnp.zeros_like(stage_low)
         for f in range(16):
             stage[f * 32:(f + 1) * 32, :] = gathered_ref[f, t * 32:(t + 1) * 32, :]
             stage_low[f * 32:f * 32 + kept, :] = gathered_ref[f, 192 + t * 32:192 + t * 32 + kept, :]
-        vector[t * 128:(t + 1) * 128, :] = dot_nt(eye, stage[...]) + dot_nt(eye, stage_low[...])
-    start_ref[...] = vector[...]
-    for f in range(16):
-        scale_rows[f * 32:(f + 1) * 32, :] = scales_ref[f, 0:32, :]
-    scale[...] = jnp.transpose(scale_rows[...])
+        start_ref[t * 128:(t + 1) * 128, :] = dot_nt(eye, stage[...]) + dot_nt(eye, stage_low[...])
     row = arrived_ref[704:720, :].astype(F32)[0:1, :]
     spot = lax.broadcasted_iota(jnp.int32, (1, 128), 1)
     for b in range(4):
@@ -277,6 +272,16 @@
         points[b] = point_ref[b]
         points_t[b] = flip_ref[b]
         weave_point(arrived_ref[192 + b * 128:320 + b * 128, :], points, points_t, 4 + b)
+
+
+def krylov_kernel(covers, bands, squares, points, points_t, start_ref, scales_ref, prior_cat, factor_ref,
+                  moment_ref, scale,
+                  mixer, vector_cat, vector_stack, vector, image, scale_rows, model, mixed, mixed_stack, forms):
+    first_tile = lax.axis_index("dish") * 2
+    vector[...] = start_ref[...]
+    for f in range(16):
+        scale_rows[f * 32:(f + 1) * 32, :] = scales_ref[f, 0:32, :]
+    scale[...] = jnp.transpose(scale_rows[...])
     factor = factor_ref[0:1, 0:1]
     build_mixer(covers, bands, squares, mixer)
 
@@ -459,21 +464,28 @@
     )(own, square, arrived, precond)
     over_freq = lax.all_gather(packed, "freq", axis=0)
     whole = (256, 512)
-    moments, covers, scale, squares, points, points_t, first = pl.pallas_call(
+    covers, squares, points, points_t, first = pl.pallas_call(
+        assemble_kernel,
+        out_shape=(shape((8,), jnp.int32), shape((8, 128, 512), BF16),
+                   shape((8, 128, 256), BF16), shape((8, 128, 256), BF16), shape(whole, F32)),
+        in_specs=[SMEM] + [VMEM] * 4,
+        out_specs=(SMEM,) + (VMEM,) * 4,
+        scratch_shapes=[pltpu.VMEM((512, 128), BF16), pltpu.VMEM((512, 128), BF16)],
+        cost_estimate=pl.CostEstimate(flops=300_000_000, bytes_accessed=4_000_000, transcendentals=0),
+        name="assemble",
+    )(coverage, over_freq, points, points_t, arrived)
+    moments, scale = pl.pallas_call(
         krylov_kernel,
-        out_shape=(shape((32, 8, 128), F32), shape((8,), jnp.int32), shape(whole, F32), shape((8, 128, 512), BF16),
-                   shape((8, 128, 256), BF16), shape((8, 128, 256), BF16), shape(whole, F32)),
+        out_shape=(shape((32, 8, 128), F32), shape(whole, F32)),
         in_specs=[SMEM] + [VMEM] * 8,
-        out_specs=(VMEM, SMEM) + (VMEM,) * 5,
+        out_specs=(VMEM, VMEM),
         scratch_shapes=[
-            pltpu.VMEM((8, DIAGS, 128, 512), F32),
+            pltpu.VMEM((8, 4, DIAGS * 128, 128), F32),
             pltpu.VMEM((256, 1536), BF16),
             pltpu.VMEM((2, 256, 512), BF16),
             pltpu.VMEM(whole, F32),
             pltpu.VMEM(whole, F32),
             pltpu.VMEM((512, 256), F32),
-            pltpu.VMEM((512, 128), BF16),
-            pltpu.VMEM((512, 128), BF16),
             pltpu.VMEM((128, 512), F32),
             pltpu.VMEM((128, 512), F32),
             pltpu.VMEM(whole, BF16),
@@ -481,7 +493,7 @@
         ],
         compiler_params=pltpu.CompilerParams(vmem_limit_bytes=54 * 1024 * 1024),
         name="krylov",
-    )(coverage, bands, over_freq, spread, prior_cat, points, points_t, factor, arrived)
+    )(covers, bands, squares, points, points_t, first, spread, prior_cat, factor)
     shared = lax.all_to_all(moments, ("tm", "dish"), split_axis=0, concat_axis=0)
     return tuple(pl.pallas_call(
         replay_kernel,
@@ -489,7 +501,7 @@
         in_specs=[SMEM] + [VMEM] * 10,
         out_specs=(VMEM, VMEM),
         scratch_shapes=[
-            pltpu.VMEM((8, DIAGS, 128, 512), F32),
+            pltpu.VMEM((8, 4, DIAGS * 128, 128), F32),
             pltpu.VMEM((256, 1536), BF16),
             pltpu.VMEM(whole, F32),
             pltpu.VMEM(whole, F32),

time: 146 us -> 145 us (level)
  the two profiles are of different devices: /device:TPU:7 before, /device:TPU:1 now
where the time goes in v2:
time: 145 us
  blocking collectives  67.9 us (47%)
  Pallas kernels  55.7 us (38%)
  between operations  14 us (10%)
  starting transfers between devices  4.17 us (3%)
  other arithmetic  1.46 us (1%)
    all_gather x1, blocking collectives, body(): over_freq = lax.all_gather(packed, 'freq', axis=0)  39.6 us
    pallas_call x1, Pallas kernels, body(): pl.pallas_call(replay_kernel, out_shape=(shape((32, 256), F32), shape((32...  20.8 us
    pallas_call x1, Pallas kernels, body(): pl.pallas_call(krylov_kernel, out_shape=(shape((32, 8, 128), F32), shape(...  19.6 us
    all_to_all x1, blocking collectives, body(): lax.all_to_all(moments, ('tm', 'dish'), split_axis=0, concat_axis=0)  14.8 us
    all_gather x1, blocking collectives, body(): over_dish = lax.all_gather(packed, 'dish', axis=0)  13.5 us
    pallas_call x1, Pallas kernels, body(): pl.pallas_call(assemble_kernel, out_shape=(shape((8,), jnp.int32), shape(...  5.29 us
    ppermute x1, starting transfers between devices, body(): lax.ppermute(ahead, 'tm', [(i, (i + 1) % count) for i in range(count)])  4.13 us
    pallas_call x1, Pallas kernels, body(): pl.pallas_call(setup_kernel, out_shape=(shape((1536, 512), BF16), shape((...  3.58 us
  transfers between devices with their start and end apart: 2, of which 1 were waited for; matrix products, arithmetic and copies ran while one was open for 0% of the time, Pallas kernels for 11%

profile of v2, /device:TPU:1, one launch (start us, length us, event | category | flops | bytes accessed | tf_op | source)
XLA Modules:
  0.0 145.1 jit_solution(15760128731232589304)
XLA Ops:
  7.2 0.0 all-gather.6.cloned.1.call-start
  7.2 1.5 %pad_maximum_fusion = f32[64,256]{1,0:T(8,128)} fusion(f32[32,256]{1,0:T(8,128)} %scale_ref.1), kind=kLoop, calls=%fused_computation | loop fusion | flops 16384 | bytes 98304 | tf_op jit(solution)/shard_map/concatenate | solution.py:430
  8.7 0.0 all-gather.6.cloned.1.call-update
  8.7 2.9 %prepare.1 = bf16[592,128]{1,0:T(8,128)(2,1)} custom-call(bf16[16,32,512]{2,1,0:T(8,128)(2,1)} %data_ref.1, bf16[16,128,128]{2,1,0:T(8,128)(2,1)} %noise_ref.1, f32[16,4,32]{2,1,0:T(4,128)} %bitcast.8), custom_call_target="tpu_custom_call" | custom-call | tf_op jit(solution)/shard_map/prepare/pallas_call | solution.py:431
  11.6 13.5 %all-gather = bf16[2368,128]{1,0:T(8,128)(2,1)} all-gather(bf16[592,128]{1,0:T(8,128)(2,1)} %prepare.1), channel_id=2, replica_groups=mesh['tm'=8,'freq'=16,'dish'=4] {'dish'}, dimensions={0}, use_global_device_ids=true | all-gather | bytes 757760 | tf_op jit(solution)/shard_map/all_gather | solution.py:439
  25.1 2.0 %project.1 = (f32[64,128]{1,0:T(8,128)}, bf16[64,128]{1,0:T(8,128)(2,1)}, bf16[720,128]{1,0:T(8,128)(2,1)}) custom-call(s32[4]{0:T(128)} %cover_ref.3, bf16[4,592,128]{2,1,0:T(8,128)(2,1)} %bitcast.4, bf16[4,128,128]{2,1,0:T(8,128)(2,1)} %point_ref.3), custom_call_target="tpu_custom_call" | custom-call | tf_op jit(solution)/shard_map/project/pallas_call | solution.py:440
  27.1 4.1 %collective-permute-start = (bf16[720,128]{1,0:T(8,128)(2,1)}, bf16[720,128]{1,0:T(8,128)(2,1)S(1)}, u32[]{:S(2)}, u32[]{:S(2)}) collective-permute-start(bf16[720,128]{1,0:T(8,128)(2,1)} %get-tuple-element.21), channel_id=1, source_target_pairs={{0,64},{64,128},{128,192},{192,256},{256,320},{320,384},{384,448},... | collective-permute-start | bytes 552968 | tf_op jit(solution)/shard_map/ppermute | solution.py:448
  31.2 3.6 %setup.1 = (bf16[1536,512]{1,0:T(8,128)(2,1)}, bf16[2176,128]{1,0:T(8,128)(2,1)}, bf16[4,128,256]{2,1,0:T(8,128)(2,1)}, bf16[4,128,256]{2,1,0:T(8,128)(2,1)}, f32[8,128]{1,0:T(8,128)}) custom-call(bf16[4,592,128]{2,1,0:T(8,128)(2,1)} %bitcast.5, f32[512,512]{1,0:T(8,128)} %prior_ref.1, bf16[4,128,128]{2,1,0:T(8,128)(2,1)} %point_ref.3), custom_call_target="tpu_custom_call" | custom-call | flops 200000000 | bytes 6000000 | tf_op jit(solution)/shard_map/setup/pallas_call | solution.py:449
  34.8 1.1 collective-permute-done.arrived_ref
  35.9 0.0 copy-start
  35.9 0.7 copy-done
  36.5 1.6 %start.1 = (f32[32,256]{1,0:T(8,128)}, bf16[254,128]{1,0:T(8,128)(2,1)}) custom-call(f32[64,128]{1,0:T(8,128)} %get-tuple-element.19.own_ref, bf16[64,128]{1,0:T(8,128)(2,1)} %get-tuple-element.20.square_ref, bf16[720,128]{1,0:T(8,128)(2,1)} %copy-done, f32[32,256]{1,0:T(8,128)} %scale_ref.1), custom_call_target="tpu_custom_call" | custom-call | tf_op jit(solution)/shard_map/start/pallas_call | solution.py:458
  38.1 39.6 %all-gather.3.gathered_ref = bf16[16,254,128]{2,1,0:T(8,128)(2,1)} all-gather(bf16[1,254,128]{2,1,0:T(8,128)(2,1)} %bitcast.7), channel_id=3, replica_groups=mesh['tm'=8,'freq'=16,'dish'=4] {'freq'}, dimensions={0}, use_global_device_ids=true | all-gather | bytes 1105408 | tf_op jit(solution)/shard_map/all_gather | solution.py:465
  77.8 5.3 %assemble.1 = (s32[8]{0:T(128)}, bf16[8,128,512]{2,1,0:T(8,128)(2,1)}, bf16[8,128,256]{2,1,0:T(8,128)(2,1)}, bf16[8,128,256]{2,1,0:T(8,128)(2,1)}, f32[256,512]{1,0:T(8,128)}) custom-call(s32[4]{0:T(128)} %cover_ref.3, bf16[16,254,128]{2,1,0:T(8,128)(2,1)} %all-gather.3.gathered_ref, bf16[4,128,256]{2,1,0:T(8,128)(2,1)} %get-tuple-element.23.point_ref, ...), custom_call_target="tpu_custom_call" | custom-call | flops 300000000 | bytes 4000000 | tf_op jit(solution)/shard_map/assemble/pallas_call | solution.py:467
  83.1 0.0 all-gather.6.cloned.1.call-done
  83.1 19.6 %krylov.1 = (f32[32,8,128]{2,1,0:T(8,128)}, f32[256,512]{1,0:T(8,128)}) custom-call(s32[8]{0:T(128)} %get-tuple-element.25.covers, bf16[2176,128]{1,0:T(8,128)(2,1)} %get-tuple-element.26.bands, bf16[8,128,512]{2,1,0:T(8,128)(2,1)} %get-tuple-element.27.squares, bf16[8,128,256]{2,1,0:T(8,128)(2,1)} %get-tuple-element.28.points, ...), custom_call_target="tpu_custom_call" | custom-call | tf_op jit(solution)/shard_map/krylov/pallas_call | solution.py:477
  102.6 14.8 %all_to_all.5.moments_ref = f32[32,8,128]{2,1,0:T(8,128)} all-to-all(f32[32,8,128]{2,1,0:T(8,128)} %get-tuple-element.33), channel_id=1, replica_groups=mesh['tm'=8,'freq'=16,'dish'=4] {'tm','dish'}, dimensions={0} | all-to-all | bytes 262144 | tf_op jit(solution)/shard_map/all_to_all | solution.py:497
  117.4 20.8 %replay.1 = (f32[32,256]{1,0:T(8,128)}, f32[32,256]{1,0:T(8,128)}) custom-call(s32[8]{0:T(128)} %get-tuple-element.25.covers, f32[32,8,128]{2,1,0:T(8,128)} %all_to_all.5.moments_ref, f32[8,128]{1,0:T(8,128)} %get-tuple-element.32.factor_ref, bf16[2176,128]{1,0:T(8,128)(2,1)} %get-tuple-element.26.bands, bf16[8,128,512]{2,1,0:T(8,128)(2,1)} %get-tuple-element.27.squares, ...), custom_call_target="tpu_custom_call" | custom-call | tf_op jit(solution)/shard_map/replay/pallas_call | solution.py:498
Async XLA Ops:
  7.2 75.9 %all-gather.6.cloned.1.call-start = ((), (), s32[]{:S(2)}) async-start(), calls=%async_computation.1 | async-start | bytes 1114112 | tf_op jit(solution)/shard_map/all_gather | solution.py:430
  27.1 8.8 %collective-permute-start = (bf16[720,128]{1,0:T(8,128)(2,1)}, bf16[720,128]{1,0:T(8,128)(2,1)S(1)}, u32[]{:S(2)}, u32[]{:S(2)}) collective-permute-start(bf16[720,128]{1,0:T(8,128)(2,1)} %get-tuple-element.21), channel_id=1, source_target_pairs={{0,64},{64,128},{128,192},{192,256},{256,320},{320,384},{384,448},... | collective-permute-start | bytes 552968 | tf_op jit(solution)/shard_map/ppermute | solution.py:448
  35.9 0.7 copy-start
Sparse Core Ops, SparseCore 0:
  10.1 67.8 all-gather.5

commit v3 on v2

--- a/solution.py
+++ b/solution.py
@@ -434,6 +434,7 @@
         in_specs=[VMEM, VMEM, VMEM],
         out_specs=VMEM,
         scratch_shapes=[pltpu.VMEM((512, 128), F32)],
+        compiler_params=pltpu.CompilerParams(vmem_limit_bytes=10 * 1024 * 1024),
         name="prepare",
     )(time_data, noise_inv, jnp.swapaxes(gains, 1, 2))
     over_dish = lax.all_gather(packed, "dish", axis=0)
@@ -442,6 +443,7 @@
         out_shape=(shape((64, 128), F32), shape((64, 128), BF16), shape((720, 128), BF16)),
         in_specs=[SMEM, VMEM, VMEM],
         out_specs=(VMEM, VMEM, VMEM),
+        compiler_params=pltpu.CompilerParams(vmem_limit_bytes=6 * 1024 * 1024),
         name="project",
     )(coverage, over_dish, pointing)
     count = lax.axis_size("tm")
@@ -453,6 +455,7 @@
         in_specs=[VMEM] * 3,
         out_specs=(VMEM,) * 5,
         cost_estimate=pl.CostEstimate(flops=200_000_000, bytes_accessed=6_000_000, transcendentals=0),
+        compiler_params=pltpu.CompilerParams(vmem_limit_bytes=14 * 1024 * 1024),
         name="setup",
     )(over_dish, prior_inv, pointing)
     right, packed = pl.pallas_call(
@@ -460,6 +463,7 @@
         out_shape=(shape((32, 256), F32), shape((SENT, 128), BF16)),
         in_specs=[VMEM] * 4,
         out_specs=(VMEM, VMEM),
+        compiler_params=pltpu.CompilerParams(vmem_limit_bytes=4 * 1024 * 1024),
         name="start",
     )(own, square, arrived, precond)
     over_freq = lax.all_gather(packed, "freq", axis=0)
@@ -472,6 +476,7 @@
         out_specs=(SMEM,) + (VMEM,) * 4,
         scratch_shapes=[pltpu.VMEM((512, 128), BF16), pltpu.VMEM((512, 128), BF16)],
         cost_estimate=pl.CostEstimate(flops=300_000_000, bytes_accessed=4_000_000, transcendentals=0),
+        compiler_params=pltpu.CompilerParams(vmem_limit_bytes=12 * 1024 * 1024),
         name="assemble",
     )(coverage, over_freq, points, points_t, arrived)
     moments, scale = pl.pallas_call(
@@ -491,7 +496,7 @@
             pltpu.VMEM(whole, BF16),
             pltpu.VMEM((8, 128), F32),
         ],
-        compiler_params=pltpu.CompilerParams(vmem_limit_bytes=54 * 1024 * 1024),
+        compiler_params=pltpu.CompilerParams(vmem_limit_bytes=50 * 1024 * 1024),
         name="krylov",
     )(covers, bands, squares, points, points_t, first, spread, prior_cat, factor)
     shared = lax.all_to_all(moments, ("tm", "dish"), split_axis=0, concat_axis=0)
@@ -511,7 +516,7 @@
             pltpu.VMEM((128, 512), F32),
             pltpu.VMEM((128, 512), F32),
         ],
-        compiler_params=pltpu.CompilerParams(vmem_limit_bytes=54 * 1024 * 1024),
+        compiler_params=pltpu.CompilerParams(vmem_limit_bytes=50 * 1024 * 1024),
         name="replay",
     )(covers, shared, factor, bands, squares, points, points_t, prior_cat, first, scale, right))
 

time: 145 us -> 145 us (level)
  the two profiles are of different devices: /device:TPU:1 before, /device:TPU:7 now
where the time goes in v3:
time: 145 us; the launch traced here: 142 us
  blocking collectives  69.9 us (48%)
  Pallas kernels  43.8 us (30%)
  between operations  14.1 us (10%)
  starting transfers between devices  5.48 us (4%)
  local copies, waits for them, and re-layouts  4.04 us (3%)
  waiting for transfers between devices  3.44 us (2%)
  other arithmetic  1.49 us (1%)
    all_gather x1, blocking collectives, body(): over_freq = lax.all_gather(packed, 'freq', axis=0)  38.7 us
    all_to_all x1, blocking collectives, body(): lax.all_to_all(moments, ('tm', 'dish'), split_axis=0, concat_axis=0)  21.2 us
    pallas_call x1, Pallas kernels, body(): pl.pallas_call(replay_kernel, out_shape=(shape((32, 256), F32), shape((32...  19.7 us
    pallas_call x1, Pallas kernels, body(): pl.pallas_call(krylov_kernel, out_shape=(shape((32, 8, 128), F32), shape(...  17.8 us
    all_gather x1, blocking collectives, body(): over_dish = lax.all_gather(packed, 'dish', axis=0)  10.1 us
    ppermute x1, starting transfers between devices, body(): lax.ppermute(ahead, 'tm', [(i, (i + 1) % count) for i in range(count)])  5.44 us
    unnamed x16, local copies, waits for them, and re-layouts  4.04 us
    pallas_call x1, Pallas kernels, body(): pl.pallas_call(assemble_kernel, out_shape=(shape((8,), jnp.int32), shape(...  3.45 us
  transfers between devices with their start and end apart: 2, of which 2 were waited for; matrix products, arithmetic and copies ran while one was open for 0% of the time, Pallas kernels for 4%

profile of v3, /device:TPU:7, one launch (start us, length us, event | category | flops | bytes accessed | tf_op | source)
XLA Modules:
  0.0 142.2 jit_solution(8118015098316629517)
XLA Ops:
  7.2 0.0 copy-start.2
  7.2 0.0 copy-start.1
  7.2 0.0 all-gather.6.cloned.1.call-start
  7.2 1.5 %pad_maximum_fusion = f32[64,256]{1,0:T(8,128)} fusion(f32[32,256]{1,0:T(8,128)} %scale_ref.1), kind=kLoop, calls=%fused_computation | loop fusion | flops 16384 | bytes 98304 | tf_op jit(solution)/shard_map/concatenate | solution.py:430
  8.7 0.0 all-gather.6.cloned.1.call-update
  8.7 0.0 copy-start.3
  8.8 1.0 copy-done.3
  9.8 0.0 copy-start.4
  9.8 1.0 copy-done.4
  10.8 0.0 copy-start.6
  10.8 0.8 copy-done.6
  11.6 0.0 copy-start.7
  11.6 1.1 prepare.1
  12.7 0.0 copy-start.5
  12.7 10.1 %all-gather = bf16[2368,128]{1,0:T(8,128)(2,1)S(1)} all-gather(bf16[592,128]{1,0:T(8,128)(2,1)S(1)} %prepare.1), channel_id=2, replica_groups=mesh['tm'=8,'freq'=16,'dish'=4] {'dish'}, dimensions={0}, use_global_device_ids=true | all-gather | bytes 757760 | tf_op jit(solution)/shard_map/all_gather | solution.py:440
  22.7 0.0 copy-done.2
  22.7 0.0 copy-done.7
  22.7 0.7 project.1
  23.5 5.4 %collective-permute-start = (bf16[720,128]{1,0:T(8,128)(2,1)S(1)}, bf16[720,128]{1,0:T(8,128)(2,1)S(1)}, u32[]{:S(2)}, u32[]{:S(2)}) collective-permute-start(bf16[720,128]{1,0:T(8,128)(2,1)S(1)} %get-tuple-element.21), channel_id=1, source_target_pairs={{0,64},{64,128},{128,192},{192,256},{256,320},{320,384},{384,448},... | collective-permute-start | bytes 552968 | tf_op jit(solution)/shard_map/ppermute | solution.py:450
  28.9 0.0 copy-done.1
  28.9 1.0 setup.1
  29.9 0.0 copy-start
  29.9 1.2 copy-done
  31.1 0.3 collective-permute-done.arrived_ref
  31.4 0.0 copy-done.5
  31.4 38.7 %all-gather.3.gathered_ref = bf16[16,254,128]{2,1,0:T(8,128)(2,1)S(1)} all-gather(bf16[1,254,128]{2,1,0:T(8,128)(2,1)S(1)} %bitcast.6), channel_id=3, replica_groups=mesh['tm'=8,'freq'=16,'dish'=4] {'freq'}, dimensions={0}, use_global_device_ids=true | all-gather | bytes 1105408 | tf_op jit(solution)/shard_map/all_gather | solution.py:469
  70.1 3.5 %assemble.1 = (s32[8]{0:T(128)S(1)}, bf16[8,128,512]{2,1,0:T(8,128)(2,1)S(1)}, bf16[8,128,256]{2,1,0:T(8,128)(2,1)S(1)}, bf16[8,128,256]{2,1,0:T(8,128)(2,1)S(1)}, f32[256,512]{1,0:T(8,128)S(1)}) custom-call(s32[4]{0:T(128)S(1)} %copy-done.7, bf16[16,254,128]{2,1,0:T(8,128)(2,1)S(1)} %all-gather.3.gathered_ref, ...), custom_call_target="tpu_custom_call" | custom-call | flops 300000000 | bytes 4000000 | tf_op jit(solution)/shard_map/assemble/pallas_call | solution.py:471
  73.5 3.1 %all-gather.6.cloned.1.call-done = f32[1024,256]{1,0:T(8,128)} async-done(((f32[64,256]{1,0:T(8,128)}), f32[1024,256]{1,0:T(8,128)}) %all-gather.6.cloned.1.call-update) | async-done | bytes 1048592 | tf_op jit(solution)/shard_map/all_gather | solution.py:430
  76.7 17.8 %krylov.1 = (f32[32,8,128]{2,1,0:T(8,128)S(1)}, f32[256,512]{1,0:T(8,128)S(1)}) custom-call(s32[8]{0:T(128)S(1)} %get-tuple-element.25.covers, bf16[2176,128]{1,0:T(8,128)(2,1)S(1)} %get-tuple-element.26.bands, bf16[8,128,512]{2,1,0:T(8,128)(2,1)S(1)} %get-tuple-element.27.squares, bf16[8,128,256]{2,1,0:T(8,128)(2,1)S(1)} %get-tuple-element.28.points, ...), custom_call_target="tpu_custom_call" | custom-call | tf_op jit(solution)/shard_map/krylov/pallas_call | solution.py:482
  94.5 21.2 %all_to_all.5.moments_ref = f32[32,8,128]{2,1,0:T(8,128)S(1)} all-to-all(f32[32,8,128]{2,1,0:T(8,128)S(1)} %get-tuple-element.33), channel_id=1, replica_groups=mesh['tm'=8,'freq'=16,'dish'=4] {'tm','dish'}, dimensions={0} | all-to-all | bytes 262144 | tf_op jit(solution)/shard_map/all_to_all | solution.py:502
  115.6 19.7 %replay.1 = (f32[32,256]{1,0:T(8,128)}, f32[32,256]{1,0:T(8,128)}) custom-call(s32[8]{0:T(128)S(1)} %get-tuple-element.25.covers, f32[32,8,128]{2,1,0:T(8,128)S(1)} %all_to_all.5.moments_ref, f32[8,128]{1,0:T(8,128)S(1)} %get-tuple-element.32.factor_ref, bf16[2176,128]{1,0:T(8,128)(2,1)S(1)} %get-tuple-element.26.bands, ...), custom_call_target="tpu_custom_call" | custom-call | tf_op jit(solution)/shard_map/replay/pallas_call | solution.py:503
  (1 shorter events, 0.0 us)
Async XLA Ops:
  7.2 15.6 %copy-start.2 = (bf16[4,128,128]{2,1,0:T(8,128)(2,1)S(1)}, bf16[4,128,128]{2,1,0:T(8,128)(2,1)}, u32[]{:S(2)}) copy-start(bf16[4,128,128]{2,1,0:T(8,128)(2,1)} %point_ref.3) | copy-start | bytes 393220
  7.2 21.7 %copy-start.1 = (f32[512,512]{1,0:T(8,128)S(1)}, f32[512,512]{1,0:T(8,128)}, u32[]{:S(2)}) copy-start(f32[512,512]{1,0:T(8,128)} %prior_ref.1) | copy-start | bytes 3145732
  7.2 69.5 %all-gather.6.cloned.1.call-start = ((), (), s32[]{:S(2)}) async-start(), calls=%async_computation.1 | async-start | bytes 1114112 | tf_op jit(solution)/shard_map/all_gather | solution.py:430
  8.7 1.0 copy-start.3
  9.8 1.0 copy-start.4
  10.8 0.8 copy-start.6
  11.6 11.1 %copy-start.7 = (s32[4]{0:T(128)S(1)}, s32[4]{0:T(128)}, u32[]{:S(2)}) copy-start(s32[4]{0:T(128)} %cover_ref.3) | copy-start | bytes 52
  12.7 18.7 %copy-start.5 = (f32[32,256]{1,0:T(8,128)S(1)}, f32[32,256]{1,0:T(8,128)}, u32[]{:S(2)}) copy-start(f32[32,256]{1,0:T(8,128)} %scale_ref.1) | copy-start | bytes 98308
  23.5 7.9 %collective-permute-start = (bf16[720,128]{1,0:T(8,128)(2,1)S(1)}, bf16[720,128]{1,0:T(8,128)(2,1)S(1)}, u32[]{:S(2)}, u32[]{:S(2)}) collective-permute-start(bf16[720,128]{1,0:T(8,128)(2,1)S(1)} %get-tuple-element.21), channel_id=1, source_target_pairs={{0,64},{64,128},{128,192},{192,256},{256,320},{320,384},{384,448},... | collective-permute-start | bytes 552968 | tf_op jit(solution)/shard_map/ppermute | solution.py:450
  29.9 1.2 copy-start
Sparse Core Ops, SparseCore 0:
  10.1 66.5 all-gather.5
